TPU v7x, 32 devices: a whole 2x2x4 slice. The times are simulated.
32 devices in a mesh: req: 8 (over z, y), tp: 4 (over x, core).
Axes of the slice: x: 2, y: 2, z: 4, core: 2. Of those that a mesh axis runs over, the one named last changes fastest.
Arguments:
- tokens: bfloat16 [16, 1024], P('req'), may hold values from -4 to 4
- slot_of: int32 [16], replicated, may hold values from 0 to 15, each once
- key_cache: bfloat16 [16, 1536, 1024], P('req', None, 'tp'), may hold values from -1100 to 1100
- value_cache: bfloat16 [16, 1536, 1024], P('req', None, 'tp'), may hold values from -6 to 6
- cache_len: int32 [16], P('req'), may hold values from 1 to 1536, as said below
- rel_bucket: int32 [16, 1536], P('req'), may hold values from 0 to 511
- rel_table: bfloat16 [512, 1024], P('req'), may hold values from -6 to 6
- w_query: bfloat16 [1024, 1024], P(None, 'tp'), may hold values from -0.1875 to 0.1875
- w_key: bfloat16 [1024, 1024], P(None, 'tp'), may hold values from -0.1875 to 0.1875
- w_out: bfloat16 [1024, 1024], P('tp'), may hold values from -0.1875 to 0.1875
- out_gain: float32 [1024], P('tp'), may hold values from 0.1 to 1.9
- out_bias: float32 [1024], P('tp'), may hold values from -0.5 to 0.5
Outputs:
- normed: bfloat16 [16, 1024], P('req', 'tp')
Inputs may be any that keep to these rules, and one draw needn't show every extreme that they name: slot_of names every slot exactly once. `cache_len`: some slot holds exactly 1536 live positions in every draw.
All inputs are finite; a program needn't handle non-finite values.
Results may differ from a plain program's by a relative error of at most 0.0034.
The roundings to bfloat16 on the way count: a program that leaves them out, or rounds other values in their place, can miss the bound.
Values may be sent and summed in bfloat16 or wider, within the bound.
No kernel may reach another device: no remote copies, remote signals or barrier semaphores. Data moves between devices by JAX's collectives and lax.ppermute only.
A program may use at most 64 MiB of HBM per device.

v0:
```python
import math
import jax
import jax.numpy as jnp
from jax import lax
from jax.sharding import PartitionSpec as P

HD = 64
BUCKETS = 512
MAXLEN = 1536
BLOCK = 512
epsilon = 1e-06
masked_score = -1e30


def norm_rows(matrix):
    row_mean = jnp.mean(matrix, axis=-1, keepdims=True)
    centred = matrix - row_mean
    variance = jnp.mean(centred * centred, axis=-1, keepdims=True)
    return centred * lax.rsqrt(variance + epsilon)


def project_rows(shard_rows, w_key, w_query):
    normed_rows = norm_rows(shard_rows.astype(jnp.float32)).astype(jnp.bfloat16)
    key_part = jnp.dot(normed_rows, w_key, preferred_element_type=jnp.float32).astype(jnp.bfloat16)
    query_part = jnp.dot(normed_rows, w_query, preferred_element_type=jnp.float32).astype(
        jnp.bfloat16
    )
    return jnp.concatenate((key_part, query_part), axis=1)


def block_scores(offset, key_rows, bucket_rows, query_heads, rel_key, rel_query):
    local_heads = query_heads.shape[0]
    block_keys = lax.dynamic_slice_in_dim(key_rows, offset, BLOCK, 0)
    forward = lax.dynamic_slice_in_dim(bucket_rows, offset, BLOCK, 0)
    backward = jnp.minimum(BUCKETS - forward, BUCKETS - 1)
    table_ids = jnp.arange(BUCKETS, dtype=jnp.int32)
    one_fwd = (forward[:, None] == table_ids[None, :]).astype(jnp.bfloat16)
    one_back = (backward[:, None] == table_ids[None, :]).astype(jnp.bfloat16)
    rows_fwd = jnp.dot(one_fwd, rel_key, preferred_element_type=jnp.float32).reshape(
        BLOCK, local_heads, HD
    )
    rows_back = jnp.dot(one_back, rel_query, preferred_element_type=jnp.float32).reshape(
        BLOCK, local_heads, HD
    )
    key_heads = block_keys.reshape(BLOCK, local_heads, HD)
    content = jnp.einsum("hd,jhd->hj", query_heads, key_heads, preferred_element_type=jnp.float32)
    along_key = jnp.einsum("hd,jhd->hj", query_heads.astype(jnp.float32), rows_fwd)
    against = jnp.sum(key_heads.astype(jnp.float32) * rows_back, axis=2).T
    return (content + along_key + against) * (1.0 / math.sqrt(3.0 * HD))


def attend_slot(query_own, key_rows, value_rows, bucket_rows, length, rel_key, rel_query):
    local_heads = query_own.shape[0] // HD
    query_heads = query_own.reshape(local_heads, HD)
    block_count = (length + BLOCK - 1) // BLOCK

    def block_step(block_index, buffer):
        offset = block_index * BLOCK
        block_part = block_scores(offset, key_rows, bucket_rows, query_heads, rel_key, rel_query)
        return lax.dynamic_update_slice_in_dim(buffer, block_part, offset, 1)

    scores = lax.fori_loop(
        0, block_count, block_step, jnp.full((local_heads, MAXLEN), masked_score, jnp.float32)
    )
    positions = jnp.arange(MAXLEN, dtype=jnp.int32)
    live_keys = (positions < length)[None, :]
    scores = jnp.where(live_keys, scores, masked_score)
    highest = jnp.max(scores, axis=1, keepdims=True)
    exponent = jnp.where(live_keys, jnp.exp(scores - highest), 0.0)
    weights = (exponent / jnp.sum(exponent, axis=1, keepdims=True)).astype(jnp.bfloat16)
    value_heads = value_rows.reshape(MAXLEN, local_heads, HD)
    context = jnp.einsum("hj,jhd->hd", weights, value_heads, preferred_element_type=jnp.float32)
    return context.reshape(local_heads * HD).astype(jnp.bfloat16)


def per_device(
    tokens,
    slot_of,
    key_cache,
    value_cache,
    cache_len,
    rel_bucket,
    rel_table,
    w_query,
    w_key,
    w_out,
    out_gain,
    out_bias,
):
    rows_dev = tokens.shape[0]
    col_width = w_query.shape[1]
    rel_both = project_rows(lax.all_gather(rel_table, "req", axis=0, tiled=True), w_key, w_query)
    rel_key = rel_both[:, :col_width]
    rel_query = rel_both[:, col_width:]
    queries = jnp.dot(tokens, w_query, preferred_element_type=jnp.float32).astype(jnp.bfloat16)
    all_queries = lax.all_gather(queries, "req", axis=0, tiled=True)
    first_row = lax.axis_index("req") * rows_dev
    own_rows = first_row + jnp.arange(rows_dev, dtype=jnp.int32)
    request_count = slot_of.shape[0]
    chooser = (slot_of[None, :] == own_rows[:, None]).astype(jnp.bfloat16)
    own_queries = jnp.dot(chooser, all_queries, preferred_element_type=jnp.float32).astype(
        jnp.bfloat16
    )
    contexts = []
    for slot_index in range(rows_dev):
        contexts.append(
            attend_slot(
                own_queries[slot_index],
                key_cache[slot_index],
                value_cache[slot_index],
                rel_bucket[slot_index],
                cache_len[slot_index],
                rel_key,
                rel_query,
            )
        )
    own_context = jnp.stack(contexts, axis=0)
    all_contexts = lax.all_gather(own_context, "req", axis=0, tiled=True)
    own_slots = lax.dynamic_slice_in_dim(slot_of, first_row, rows_dev, 0)
    picker = (own_slots[:, None] == jnp.arange(request_count, dtype=jnp.int32)[None, :]).astype(
        jnp.bfloat16
    )
    context_rows = jnp.dot(picker, all_contexts, preferred_element_type=jnp.float32).astype(
        jnp.bfloat16
    )
    partial_out = jnp.dot(context_rows, w_out, preferred_element_type=jnp.float32)
    col_start = lax.axis_index("tp") * col_width
    row_sum = lax.psum(partial_out, "tp")
    normed_full = norm_rows(row_sum + tokens.astype(jnp.float32))
    own_cols = lax.dynamic_slice_in_dim(normed_full, col_start, col_width, 1)
    return (own_cols * out_gain + out_bias).astype(jnp.bfloat16)


def solution(mesh):
    in_specs = (
        P("req", None),
        P(),
        P("req", None, "tp"),
        P("req", None, "tp"),
        P("req"),
        P("req", None),
        P("req", None),
        P(None, "tp"),
        P(None, "tp"),
        P("tp", None),
        P("tp"),
        P("tp"),
    )
    out_specs = P("req", "tp")
    return jax.shard_map(
        per_device, mesh=mesh, in_specs=in_specs, out_specs=out_specs, check_vma=False
    )
```

profile of v0, /device:TPU:0, one launch (start us, length us, event | category | flops | bytes accessed | tf_op | source)
XLA Modules:
  0.0 98.8 jit_solution(9995086282330034420)
XLA Ops:
  6.5 0.7 all-gather.4.cloned.1.call-update
  7.3 1.4 %fusion.53 = (s32[1]{0:T(128)}, s32[1]{0:T(128)}) fusion(s32[2]{0:T(128)} %param.20), kind=kLoop, calls=%fused_computation.89 | loop fusion | bytes 16 | tf_op jit(solution)/shard_map/slice | solution.py:112
  10.1 0.9 fusion.25
  10.9 22.3 %all-gather = bf16[8,2,256]{2,1,0:T(2,128)(2,1)S(1)} all-gather(bf16[1,2,256]{2,1,0:T(2,128)(2,1)S(1)} %fusion.25), channel_id=1, replica_groups=mesh['req'=8,'tp'=4] {'req'}, dimensions={0}, use_global_device_ids=true | all-gather | bytes 9216 | tf_op jit(solution)/shard_map/all_gather | solution.py:96
  33.2 0.7 dynamic_slice.18
  33.9 0.8 convolution_convert_fusion.4
  34.8 0.1 reshape_squeeze.12
  34.9 0.1 reshape_squeeze.14
  35.0 1.5 %fusion.51 = (bf16[1,1536,256]{2,1,0:T(8,128)(2,1)S(1)}, bf16[1,1536,256]{2,1,0:T(8,128)(2,1)S(1)}) fusion(bf16[2,1536,256]{2,1,0:T(8,128)(2,1)} %param.18), kind=kLoop, calls=%fused_computation.87 | loop fusion | bytes 3145728 | tf_op jit(solution)/shard_map/slice | solution.py:109
  36.5 1.2 %copy.33 = bf16[1,1536,256]{1,2,0:T(8,128)(2,1)} copy(bf16[1,1536,256]{2,1,0:T(8,128)(2,1)S(1)} %get-tuple-element.139) | data formatting | bytes 1572864
  37.6 1.2 %copy.35 = bf16[1,1536,256]{1,2,0:T(8,128)(2,1)} copy(bf16[1,1536,256]{2,1,0:T(8,128)(2,1)S(1)} %get-tuple-element.140) | data formatting | bytes 1572864
  38.8 1.5 %fusion.52 = (bf16[1,1536,256]{2,1,0:T(8,128)(2,1)S(1)}, bf16[1,1536,256]{2,1,0:T(8,128)(2,1)S(1)}) fusion(bf16[2,1536,256]{2,1,0:T(8,128)(2,1)} %param.19), kind=kLoop, calls=%fused_computation.88 | loop fusion | bytes 3145728 | tf_op jit(solution)/shard_map/slice | solution.py:110
  40.3 0.3 copy.34
  40.6 0.3 copy.36
  40.9 0.7 iota_compare_fusion.9
  41.6 0.7 iota_compare_fusion.8
  42.3 10.1 %all-gather.4.cloned.1.call-done = bf16[512,1024]{1,0:T(8,128)(2,1)} async-done(((bf16[64,1024]{1,0:T(8,128)(2,1)}), bf16[512,1024]{1,0:T(8,128)(2,1)}) %all-gather.4.cloned.1.call-update) | async-done | bytes 1048592 | tf_op jit(solution)/shard_map/all_gather | solution.py:92
  52.5 1.5 %convert_reduce_fusion = f32[512]{0:T(512)S(1)} fusion(bf16[512,1024]{1,0:T(8,128)(2,1)} %all-gather.4.cloned.1.call-done), kind=kLoop, calls=%fused_computation.35 | loop fusion | flops 1048064 | bytes 1050624 | tf_op jit(solution)/shard_map/reduce_sum | solution.py:16
  54.0 0.4 fusion.22
  54.4 0.5 convolution_convert_fusion
  54.9 0.5 copy-done.7
  55.5 0.5 convolution_convert_fusion.1
  56.0 2.4 %while.20 = (s32[]{:T(128)}, f32[4,1536]{1,0:T(4,128)S(1)}, s32[]{:T(128)}, bf16[1536,256]{0,1:T(8,128)(2,1)}, bf16[4,64]{1,0:T(4,128)(2,1)S(1)}, /*index=5*/s32...) while((s32[]{:T(128)}, f32[4,1536]{1,0:T(4,128)S(1)}, ...), condition=%wide.region_4.5_spmd, body=%wide.region_2.4_spmd.sunk | while | flops 269882368 | bytes 1903791 | solution.py:62
  56.1 0.5 fusion.97
  56.6 0.1 fusion.98
  56.7 1.5 %multiply_reduce_fusion.5 = (f32[512,4]{0,1:T(4,128)S(1)}, bf16[512,256]{0,1:T(8,128)(2,1)S(1)}) fusion(bf16[1536,256]{0,1:T(8,128)(2,1)} %get-tuple-element.324, s32[]{:T(128)S(6)} %select_n.77, bf16[512,256]{1,0:T(8,128)(2,1)S(1)} %get-tuple-element.328, s32[512]{0:T(512)S(1)} %get-tuple-element.245), kind=kOutput, calls=%fused_computation.4.clone.1 | convolution fusion | flops 134871040 | bytes 796676 | tf_op jit(solution)/shard_map/while/body/dot_general | solution.py:42
  58.2 0.1 fusion.99
  58.4 0.1 select_reduce_fusion.1
  58.5 0.2 fusion.30
  58.7 0.1 fusion.32
  58.8 2.4 %while.21 = (s32[]{:T(128)}, f32[4,1536]{1,0:T(4,128)S(1)}, s32[]{:T(128)}, bf16[1536,256]{0,1:T(8,128)(2,1)}, bf16[4,64]{1,0:T(4,128)(2,1)S(1)}, /*index=5*/s32...) while((s32[]{:T(128)}, f32[4,1536]{1,0:T(4,128)S(1)}, ...), condition=%wide.region_9.10_spmd, body=%wide.region_7.9_spmd.sunk | while | flops 269882368 | bytes 1903791 | solution.py:62
  58.9 0.5 fusion.107
  59.4 0.1 fusion.108
  59.6 1.5 %multiply_reduce_fusion.6 = (f32[512,4]{0,1:T(4,128)S(1)}, bf16[512,256]{0,1:T(8,128)(2,1)S(1)}) fusion(bf16[1536,256]{0,1:T(8,128)(2,1)} %get-tuple-element.288, s32[]{:T(128)S(6)} %select_n.78, bf16[512,256]{1,0:T(8,128)(2,1)S(1)} %get-tuple-element.292, s32[512]{0:T(512)S(1)} %get-tuple-element.257), kind=kOutput, calls=%fused_computation.21.clone.1 | convolution fusion | flops 134871040 | bytes 796676 | tf_op jit(solution)/shard_map/while/body/dot_general | solution.py:42
  61.1 0.1 fusion.109
  61.3 0.1 select_reduce_fusion
  61.4 0.2 fusion.31
  61.6 0.1 fusion.33
  61.7 0.3 fusion.28
  62.0 0.1 convert_element_type.81
  62.1 0.3 fusion.26
  62.4 0.1 convert_element_type.84
  62.6 22.3 %all-gather.1 = bf16[8,2,256]{2,1,0:T(2,128)(2,1)S(1)} all-gather(bf16[1,2,256]{2,1,0:T(2,128)(2,1)S(1)} %maximum_bitcast_fusion), channel_id=1, replica_groups=mesh['req'=8,'tp'=4] {'req'}, dimensions={0}, use_global_device_ids=true | all-gather | bytes 9216 | tf_op jit(solution)/shard_map/all_gather | solution.py:118
  84.9 0.3 fusion.24
  85.2 5.7 %psum.7 = f32[2,1024]{1,0:T(2,128)S(1)} all-reduce(f32[2,1024]{1,0:T(2,128)S(1)} %fusion.24), channel_id=1, replica_groups=mesh['req'=8,'tp'=4] {'tp'}, use_global_device_ids=true, to_apply=%region_12.13 | all-reduce | flops 2048 | bytes 16384 | tf_op jit(solution)/shard_map/psum | solution.py:128
  91.0 0.1 fusion.35
  91.1 0.2 multiply_reduce_fusion.2
  91.3 0.6 fusion.38
  (34 shorter events, 0.4 us)
Async XLA Ops:
  6.5 3.5 %copy-start = (bf16[1024,256]{1,0:T(8,128)(2,1)S(1)}, bf16[1024,256]{1,0:T(8,128)(2,1)}, u32[]{:S(2)}) copy-start(bf16[1024,256]{1,0:T(8,128)(2,1)} %param.23) | copy-start | bytes 1572868
  6.5 45.9 %all-gather.4.cloned.1.call-start = ((), (), s32[]{:S(2)}) async-start(), calls=%async_computation | async-start | bytes 1179648 | tf_op jit(solution)/shard_map/all_gather | solution.py:92
  40.3 2.0 %copy-start.4 = (s32[2,1536]{1,0:T(2,128)S(1)}, s32[2,1536]{1,0:T(2,128)}, u32[]{:S(2)}) copy-start(s32[2,1536]{1,0:T(2,128)} %param.21) | copy-start | bytes 36868
  52.5 1.5 %copy-start.1 = (bf16[512,1024]{1,0:T(8,128)(2,1)S(1)}, bf16[512,1024]{1,0:T(8,128)(2,1)}, u32[]{:S(2)}) copy-start(bf16[512,1024]{1,0:T(8,128)(2,1)} %all-gather.4.cloned.1.call-done) | copy-start | bytes 3145732
  54.4 1.0 %copy-start.7 = (bf16[1024,256]{1,0:T(8,128)(2,1)S(1)}, bf16[1024,256]{1,0:T(8,128)(2,1)}, u32[]{:S(2)}) copy-start(bf16[1024,256]{1,0:T(8,128)(2,1)} %param.24) | copy-start | bytes 1572868
  61.2 23.7 %copy-start.2 = (bf16[256,1024]{1,0:T(8,128)(2,1)S(1)}, bf16[256,1024]{1,0:T(8,128)(2,1)}, u32[]{:S(2)}) copy-start(bf16[256,1024]{1,0:T(8,128)(2,1)} %param.25) | copy-start | bytes 1572868
  61.3 29.7 %copy-start.3 = (bf16[2,1024]{1,0:T(2,128)(2,1)S(1)}, bf16[2,1024]{1,0:T(2,128)(2,1)}, u32[]{:S(2)}) copy-start(bf16[2,1024]{1,0:T(2,128)(2,1)} %param.16) | copy-start | bytes 12292
  61.3 30.1 %copy-start.5 = (f32[256]{0:T(256)S(1)}, f32[256]{0:T(256)}, u32[]{:S(2)}) copy-start(f32[256]{0:T(256)} %param.27) | copy-start | bytes 3076
  61.3 30.0 %copy-start.6 = (f32[256]{0:T(256)S(1)}, f32[256]{0:T(256)}, u32[]{:S(2)}) copy-start(f32[256]{0:T(256)} %param.26) | copy-start | bytes 3076
Sparse Core Ops, SparseCore 0:
  9.5 42.9 all-gather.3
where the time goes:
time: 99.3 us; the launch traced here: 98.8 us
  blocking collectives  50.3 us (51%)
  between operations  15 us (15%)
  waiting for transfers between devices  10.9 us (11%)
  local copies, waits for them, and re-layouts  8.97 us (9%)
  matrix products  8.17 us (8%)
  other arithmetic  5.37 us (5%)
    all_gather x1, blocking collectives, per_device(): all_contexts = lax.all_gather(own_context, 'req', axis=0, tiled=True)  22.3 us
    all_gather x1, blocking collectives, per_device(): all_queries = lax.all_gather(queries, 'req', axis=0, tiled=True)  22.3 us
    all_gather x1, waiting for transfers between devices, per_device(): lax.all_gather(rel_table, 'req', axis=0, tiled=True)  10.1 us
    psum x1, blocking collectives, per_device(): row_sum = lax.psum(partial_out, 'tp')  5.75 us
    unnamed x22, local copies, waits for them, and re-layouts  3.5 us
    dot_general x2, matrix products, block_scores(): jnp.dot(one_back, rel_query, preferred_element_type=jnp.float32)  2.97 us
  transfers between devices with their start and end apart: 1, of which 1 were waited for; matrix products, arithmetic and copies ran while one was open for 11% of the time, Pallas kernels for 0%

commit v1 on v0

--- a/solution.py
+++ b/solution.py
@@ -10,6 +10,24 @@
 BLOCK = 512
 epsilon = 1e-06
 masked_score = -1e30
+
+
+def collect(shard, axis, dim):
+    ways, here, step = (lax.axis_size(axis), lax.axis_index(axis), shard.shape[dim])
+    shape = [n * ways if d == dim else n for d, n in enumerate(shard.shape)]
+    full = lax.dynamic_update_slice_in_dim(
+        jnp.zeros(shape, shard.dtype), shard, here * step, axis=dim
+    )
+    going_up = going_down = shard
+    for far in range(1, ways // 2 + 1):
+        going_up = lax.ppermute(going_up, axis, [(d, (d + 1) % ways) for d in range(ways)])
+        full = lax.dynamic_update_slice_in_dim(full, going_up, (here - far) % ways * step, axis=dim)
+        if 2 * far < ways:
+            going_down = lax.ppermute(going_down, axis, [(d, (d - 1) % ways) for d in range(ways)])
+            full = lax.dynamic_update_slice_in_dim(
+                full, going_down, (here + far) % ways * step, axis=dim
+            )
+    return full
 
 
 def norm_rows(matrix):
@@ -115,7 +133,7 @@
             )
         )
     own_context = jnp.stack(contexts, axis=0)
-    all_contexts = lax.all_gather(own_context, "req", axis=0, tiled=True)
+    all_contexts = collect(own_context, "req", 0)
     own_slots = lax.dynamic_slice_in_dim(slot_of, first_row, rows_dev, 0)
     picker = (own_slots[:, None] == jnp.arange(request_count, dtype=jnp.int32)[None, :]).astype(
         jnp.bfloat16

time: 99.3 us -> 103 us (1.037)
  blocking collectives: 50.3 us -> 28 us
  starting transfers between devices: 0.01 us -> 15.4 us
  waiting for transfers between devices: 10.9 us -> 21.5 us
    all_gather x1 -> x0, blocking collectives: 22.3 us -> none  [per_device(): all_contexts = lax.all_gather(own_context, 'req', axis=0, tiled=True)]
    ppermute x0 -> x7, starting transfers between devices: none -> 15.4 us  [the longest x4 7.72 us: collect(): lax.ppermute(going_up, axis, [(d, (d + 1) % ways) for d in range(ways)])]
    ppermute x0 -> x7, waiting for transfers between devices: none -> 10 us  [the longest x4 10 us: collect(): lax.ppermute(going_up, axis, [(d, (d + 1) % ways) for d in range(ways)])]
    unnamed x22 -> x23, local copies, waits for them, and re-layouts: 3.5 us -> 3.5 us
  transfers between devices with their start and end apart: 1 -> 8, of which waited for: 1 -> 5; matrix products, arithmetic and copies ran while one was open for 11% -> 10% of each run, Pallas kernels for 0% -> 0%
where the time goes in v1:
time: 103 us; the launch traced here: 102 us
  blocking collectives  28 us (27%)
  waiting for transfers between devices  21.5 us (21%)
  starting transfers between devices  15.4 us (15%)
  between operations  15.2 us (15%)
  local copies, waits for them, and re-layouts  8.39 us (8%)
  matrix products  8.16 us (8%)
  other arithmetic  5.38 us (5%)
    all_gather x1, blocking collectives, per_device(): all_queries = lax.all_gather(queries, 'req', axis=0, tiled=True)  22.3 us
    all_gather x1, waiting for transfers between devices, per_device(): lax.all_gather(rel_table, 'req', axis=0, tiled=True)  10.7 us
    ppermute x4, waiting for transfers between devices, collect(): lax.ppermute(going_up, axis, [(d, (d + 1) % ways) for d in range(ways)])  10 us
    ppermute x4, starting transfers between devices, collect(): lax.ppermute(going_up, axis, [(d, (d + 1) % ways) for d in range(ways)])  7.72 us
    ppermute x3, starting transfers between devices, collect(): lax.ppermute(going_down, axis, [(d, (d - 1) % ways) for d in range(ways)])  7.66 us
    psum x1, blocking collectives, per_device(): row_sum = lax.psum(partial_out, 'tp')  5.75 us
    unnamed x23, local copies, waits for them, and re-layouts  3.5 us
    dot_general x2, matrix products, block_scores(): jnp.dot(one_back, rel_query, preferred_element_type=jnp.float32)  2.96 us
  transfers between devices with their start and end apart: 8, of which 5 were waited for; matrix products, arithmetic and copies ran while one was open for 10% of the time, Pallas kernels for 0%

profile of v1, /device:TPU:0, one launch (start us, length us, event | category | flops | bytes accessed | tf_op | source)
XLA Modules:
  0.0 102.1 jit_solution(6528186047661797971)
XLA Ops:
  6.5 0.7 all-gather.3.cloned.1.call-update
  7.4 1.4 %fusion.54 = (s32[1]{0:T(128)}, s32[1]{0:T(128)}) fusion(s32[2]{0:T(128)} %param.20), kind=kLoop, calls=%fused_computation.98 | loop fusion | bytes 16 | tf_op jit(solution)/shard_map/slice | solution.py:130
  10.2 0.9 fusion.25
  11.1 22.3 %all-gather = bf16[8,2,256]{2,1,0:T(2,128)(2,1)S(1)} all-gather(bf16[1,2,256]{2,1,0:T(2,128)(2,1)S(1)} %fusion.25), channel_id=1, replica_groups=mesh['req'=8,'tp'=4] {'req'}, dimensions={0}, use_global_device_ids=true | all-gather | bytes 9216 | tf_op jit(solution)/shard_map/all_gather | solution.py:114
  33.3 0.8 convolution_convert_fusion.4
  34.4 1.5 %fusion.52 = (bf16[1,1536,256]{2,1,0:T(8,128)(2,1)S(1)}, bf16[1,1536,256]{2,1,0:T(8,128)(2,1)S(1)}) fusion(bf16[2,1536,256]{2,1,0:T(8,128)(2,1)} %param.18), kind=kLoop, calls=%fused_computation.96 | loop fusion | bytes 3145728 | tf_op jit(solution)/shard_map/slice | solution.py:127
  35.8 1.2 %copy.33 = bf16[1,1536,256]{1,2,0:T(8,128)(2,1)} copy(bf16[1,1536,256]{2,1,0:T(8,128)(2,1)S(1)} %get-tuple-element.141) | data formatting | bytes 1572864
  37.0 1.2 %copy.35 = bf16[1,1536,256]{1,2,0:T(8,128)(2,1)} copy(bf16[1,1536,256]{2,1,0:T(8,128)(2,1)S(1)} %get-tuple-element.142) | data formatting | bytes 1572864
  38.2 1.5 %fusion.53 = (bf16[1,1536,256]{2,1,0:T(8,128)(2,1)S(1)}, bf16[1,1536,256]{2,1,0:T(8,128)(2,1)S(1)}) fusion(bf16[2,1536,256]{2,1,0:T(8,128)(2,1)} %param.19), kind=kLoop, calls=%fused_computation.97 | loop fusion | bytes 3145728 | tf_op jit(solution)/shard_map/slice | solution.py:128
  39.7 0.3 copy.34
  40.0 0.3 copy.36
  40.3 0.7 iota_compare_fusion.9
  41.0 0.7 iota_compare_fusion.8
  41.7 10.7 %all-gather.3.cloned.1.call-done = bf16[512,1024]{1,0:T(8,128)(2,1)} async-done(((bf16[64,1024]{1,0:T(8,128)(2,1)}), bf16[512,1024]{1,0:T(8,128)(2,1)}) %all-gather.3.cloned.1.call-update) | async-done | bytes 1048592 | tf_op jit(solution)/shard_map/all_gather | solution.py:110
  52.5 1.5 %convert_reduce_fusion = f32[512]{0:T(512)S(1)} fusion(bf16[512,1024]{1,0:T(8,128)(2,1)} %all-gather.3.cloned.1.call-done), kind=kLoop, calls=%fused_computation.35 | loop fusion | flops 1048064 | bytes 1050624 | tf_op jit(solution)/shard_map/reduce_sum | solution.py:34
  54.0 0.4 fusion.22
  54.4 0.5 convolution_convert_fusion
  54.9 0.5 copy-done.7
  55.5 0.5 convolution_convert_fusion.1
  56.0 2.4 %while.20 = (s32[]{:T(128)}, f32[4,1536]{1,0:T(4,128)S(1)}, s32[]{:T(128)}, bf16[1536,256]{0,1:T(8,128)(2,1)}, bf16[4,64]{1,0:T(4,128)(2,1)S(1)}, /*index=5*/s32...) while((s32[]{:T(128)}, f32[4,1536]{1,0:T(4,128)S(1)}, ...), condition=%wide.region_4.5_spmd, body=%wide.region_2.4_spmd.sunk | while | flops 269882368 | bytes 1903791 | solution.py:80
  56.1 0.5 fusion.98
  56.6 0.1 fusion.99
  56.7 1.5 %multiply_reduce_fusion.5 = (f32[512,4]{0,1:T(4,128)S(1)}, bf16[512,256]{0,1:T(8,128)(2,1)S(1)}) fusion(bf16[1536,256]{0,1:T(8,128)(2,1)} %get-tuple-element.326, s32[]{:T(128)S(6)} %select_n.143, bf16[512,256]{1,0:T(8,128)(2,1)S(1)} %get-tuple-element.330, s32[512]{0:T(512)S(1)} %get-tuple-element.247), kind=kOutput, calls=%fused_computation.4.clone.1 | convolution fusion | flops 134871040 | bytes 796676 | tf_op jit(solution)/shard_map/while/body/dot_general | solution.py:60
  58.2 0.1 fusion.100
  58.4 0.1 select_reduce_fusion.1
  58.5 0.2 fusion.30
  58.8 2.4 %while.21 = (s32[]{:T(128)}, f32[4,1536]{1,0:T(4,128)S(1)}, s32[]{:T(128)}, bf16[1536,256]{0,1:T(8,128)(2,1)}, bf16[4,64]{1,0:T(4,128)(2,1)S(1)}, /*index=5*/s32...) while((s32[]{:T(128)}, f32[4,1536]{1,0:T(4,128)S(1)}, ...), condition=%wide.region_9.10_spmd, body=%wide.region_7.9_spmd.sunk | while | flops 269882368 | bytes 1903791 | solution.py:80
  58.9 0.5 fusion.108
  59.4 0.1 fusion.109
  59.6 1.5 %multiply_reduce_fusion.6 = (f32[512,4]{0,1:T(4,128)S(1)}, bf16[512,256]{0,1:T(8,128)(2,1)S(1)}) fusion(bf16[1536,256]{0,1:T(8,128)(2,1)} %get-tuple-element.290, s32[]{:T(128)S(6)} %select_n.144, bf16[512,256]{1,0:T(8,128)(2,1)S(1)} %get-tuple-element.294, s32[512]{0:T(512)S(1)} %get-tuple-element.259), kind=kOutput, calls=%fused_computation.21.clone.1 | convolution fusion | flops 134871040 | bytes 796676 | tf_op jit(solution)/shard_map/while/body/dot_general | solution.py:60
  61.1 0.1 fusion.110
  61.3 0.1 select_reduce_fusion
  61.4 0.2 fusion.31
  61.7 0.3 fusion.28
  62.1 0.3 fusion.26
  62.6 5.4 %collective-permute-start = (bf16[2,256]{1,0:T(2,128)(2,1)S(1)}, bf16[2,256]{1,0:T(2,128)(2,1)S(1)}, u32[]{:S(2)}, u32[]{:S(2)}) collective-permute-start(bf16[2,256]{1,0:T(2,128)(2,1)S(1)} %get-tuple-element.140), channel_id=1, source_target_pairs={{0,4},{4,8},{8,12},{12,16},{16,20},{20,24},{24,28},{28,0},{1,5},{5... | collective-permute-start | bytes 3080 | tf_op jit(solution)/shard_map/ppermute | solution.py:23
  68.1 1.2 %collective-permute-done = bf16[2,256]{1,0:T(2,128)(2,1)S(1)} collective-permute-done((bf16[2,256]{1,0:T(2,128)(2,1)S(1)}, bf16[2,256]{1,0:T(2,128)(2,1)S(1)}, u32[]{:S(2)}, u32[]{:S(2)}) %collective-permute-start) | collective-permute-done | bytes 1056 | tf_op jit(solution)/shard_map/ppermute | solution.py:23
  69.3 2.3 %collective-permute-start.2 = (bf16[2,256]{1,0:T(2,128)(2,1)S(1)}, bf16[2,256]{1,0:T(2,128)(2,1)S(1)}, u32[]{:S(2)}, u32[]{:S(2)}) collective-permute-start(bf16[2,256]{1,0:T(2,128)(2,1)S(1)} %collective-permute-done), channel_id=1, source_target_pairs={{0,4},{4,8},{8,12},{12,16},{16,20},{20,24},{24,28},{28,0},{1,5},{5... | collective-permute-start | bytes 3080 | tf_op jit(solution)/shard_map/ppermute | solution.py:23
  71.6 2.7 %collective-permute-start.3 = (bf16[2,256]{1,0:T(2,128)(2,1)S(1)}, bf16[2,256]{1,0:T(2,128)(2,1)S(1)}, u32[]{:S(2)}, u32[]{:S(2)}) collective-permute-start(bf16[2,256]{1,0:T(2,128)(2,1)S(1)} %collective-permute-done.1), channel_id=1, source_target_pairs={{0,28},{4,0},{8,4},{12,8},{16,12},{20,16},{24,20},{28,24},{1,29},{... | collective-permute-start | bytes 3080 | tf_op jit(solution)/shard_map/ppermute | solution.py:26
  74.3 1.3 %collective-permute-done.2 = bf16[2,256]{1,0:T(2,128)(2,1)S(1)} collective-permute-done((bf16[2,256]{1,0:T(2,128)(2,1)S(1)}, bf16[2,256]{1,0:T(2,128)(2,1)S(1)}, u32[]{:S(2)}, u32[]{:S(2)}) %collective-permute-start.2) | collective-permute-done | bytes 1056 | tf_op jit(solution)/shard_map/ppermute | solution.py:23
  75.6 5.0 %collective-permute-start.5 = (bf16[2,256]{1,0:T(2,128)(2,1)S(1)}, bf16[2,256]{1,0:T(2,128)(2,1)S(1)}, u32[]{:S(2)}, u32[]{:S(2)}) collective-permute-start(bf16[2,256]{1,0:T(2,128)(2,1)S(1)} %collective-permute-done.3), channel_id=1, source_target_pairs={{0,28},{4,0},{8,4},{12,8},{16,12},{20,16},{24,20},{28,24},{1,29},{... | collective-permute-start | bytes 3080 | tf_op jit(solution)/shard_map/ppermute | solution.py:26
  80.6 1.3 %collective-permute-done.4 = bf16[2,256]{1,0:T(2,128)(2,1)S(1)} collective-permute-done((bf16[2,256]{1,0:T(2,128)(2,1)S(1)}, bf16[2,256]{1,0:T(2,128)(2,1)S(1)}, u32[]{:S(2)}, u32[]{:S(2)}) %collective-permute-start.4) | collective-permute-done | bytes 1056 | tf_op jit(solution)/shard_map/ppermute | solution.py:23
  81.9 6.2 %collective-permute-done.6 = bf16[2,256]{1,0:T(2,128)(2,1)S(1)} collective-permute-done((bf16[2,256]{1,0:T(2,128)(2,1)S(1)}, bf16[2,256]{1,0:T(2,128)(2,1)S(1)}, u32[]{:S(2)}, u32[]{:S(2)}) %collective-permute-start.6) | collective-permute-done | bytes 1056 | tf_op jit(solution)/shard_map/ppermute | solution.py:23
  88.1 0.3 fusion.24
  88.4 5.7 %psum.7 = f32[2,1024]{1,0:T(2,128)S(1)} all-reduce(f32[2,1024]{1,0:T(2,128)S(1)} %fusion.24), channel_id=1, replica_groups=mesh['req'=8,'tp'=4] {'tp'}, use_global_device_ids=true, to_apply=%region_12.13 | all-reduce | flops 2048 | bytes 16384 | tf_op jit(solution)/shard_map/psum | solution.py:146
  94.2 0.1 fusion.35
  94.3 0.2 multiply_reduce_fusion.2
  94.6 0.6 fusion.39
  (56 shorter events, 1.1 us)
Async XLA Ops:
  6.5 3.6 %copy-start = (bf16[1024,256]{1,0:T(8,128)(2,1)S(1)}, bf16[1024,256]{1,0:T(8,128)(2,1)}, u32[]{:S(2)}) copy-start(bf16[1024,256]{1,0:T(8,128)(2,1)} %param.23) | copy-start | bytes 1572868
  6.5 45.9 %all-gather.3.cloned.1.call-start = ((), (), s32[]{:S(2)}) async-start(), calls=%async_computation | async-start | bytes 1179648 | tf_op jit(solution)/shard_map/all_gather | solution.py:110
  39.7 2.0 %copy-start.4 = (s32[2,1536]{1,0:T(2,128)S(1)}, s32[2,1536]{1,0:T(2,128)}, u32[]{:S(2)}) copy-start(s32[2,1536]{1,0:T(2,128)} %param.21) | copy-start | bytes 36868
  52.5 1.5 %copy-start.1 = (bf16[512,1024]{1,0:T(8,128)(2,1)S(1)}, bf16[512,1024]{1,0:T(8,128)(2,1)}, u32[]{:S(2)}) copy-start(bf16[512,1024]{1,0:T(8,128)(2,1)} %all-gather.3.cloned.1.call-done) | copy-start | bytes 3145732
  54.4 1.0 %copy-start.7 = (bf16[1024,256]{1,0:T(8,128)(2,1)S(1)}, bf16[1024,256]{1,0:T(8,128)(2,1)}, u32[]{:S(2)}) copy-start(bf16[1024,256]{1,0:T(8,128)(2,1)} %param.24) | copy-start | bytes 1572868
  61.2 6.8 %copy-start.8 = (s32[16]{0:T(128)S(1)}, s32[16]{0:T(128)}, u32[]{:S(2)}) copy-start(s32[16]{0:T(128)} %param.17) | copy-start | bytes 196
  61.2 26.9 %copy-start.2 = (bf16[256,1024]{1,0:T(8,128)(2,1)S(1)}, bf16[256,1024]{1,0:T(8,128)(2,1)}, u32[]{:S(2)}) copy-start(bf16[256,1024]{1,0:T(8,128)(2,1)} %param.25) | copy-start | bytes 1572868
  61.3 32.9 %copy-start.3 = (bf16[2,1024]{1,0:T(2,128)(2,1)S(1)}, bf16[2,1024]{1,0:T(2,128)(2,1)}, u32[]{:S(2)}) copy-start(bf16[2,1024]{1,0:T(2,128)(2,1)} %param.16) | copy-start | bytes 12292
  61.3 33.3 %copy-start.5 = (f32[256]{0:T(256)S(1)}, f32[256]{0:T(256)}, u32[]{:S(2)}) copy-start(f32[256]{0:T(256)} %param.27) | copy-start | bytes 3076
  61.3 33.3 %copy-start.6 = (f32[256]{0:T(256)S(1)}, f32[256]{0:T(256)}, u32[]{:S(2)}) copy-start(f32[256]{0:T(256)} %param.26) | copy-start | bytes 3076
  62.6 6.7 %collective-permute-start = (bf16[2,256]{1,0:T(2,128)(2,1)S(1)}, bf16[2,256]{1,0:T(2,128)(2,1)S(1)}, u32[]{:S(2)}, u32[]{:S(2)}) collective-permute-start(bf16[2,256]{1,0:T(2,128)(2,1)S(1)} %get-tuple-element.140), channel_id=1, source_target_pairs={{0,4},{4,8},{8,12},{12,16},{16,20},{20,24},{24,28},{28,0},{1,5},{5... | collective-permute-start | bytes 3080 | tf_op jit(solution)/shard_map/ppermute | solution.py:23
  68.0 3.6 %collective-permute-start.1 = (bf16[2,256]{1,0:T(2,128)(2,1)S(1)}, bf16[2,256]{1,0:T(2,128)(2,1)S(1)}, u32[]{:S(2)}, u32[]{:S(2)}) collective-permute-start(bf16[2,256]{1,0:T(2,128)(2,1)S(1)} %get-tuple-element.140), channel_id=1, source_target_pairs={{0,28},{4,0},{8,4},{12,8},{16,12},{20,16},{24,20},{28,24},{1,29},{... | collective-permute-start | bytes 3080 | tf_op jit(solution)/shard_map/ppermute | solution.py:26
  69.3 6.3 %collective-permute-start.2 = (bf16[2,256]{1,0:T(2,128)(2,1)S(1)}, bf16[2,256]{1,0:T(2,128)(2,1)S(1)}, u32[]{:S(2)}, u32[]{:S(2)}) collective-permute-start(bf16[2,256]{1,0:T(2,128)(2,1)S(1)} %collective-permute-done), channel_id=1, source_target_pairs={{0,4},{4,8},{8,12},{12,16},{16,20},{20,24},{24,28},{28,0},{1,5},{5... | collective-permute-start | bytes 3080 | tf_op jit(solution)/shard_map/ppermute | solution.py:23
  71.6 4.0 %collective-permute-start.3 = (bf16[2,256]{1,0:T(2,128)(2,1)S(1)}, bf16[2,256]{1,0:T(2,128)(2,1)S(1)}, u32[]{:S(2)}, u32[]{:S(2)}) collective-permute-start(bf16[2,256]{1,0:T(2,128)(2,1)S(1)} %collective-permute-done.1), channel_id=1, source_target_pairs={{0,28},{4,0},{8,4},{12,8},{16,12},{20,16},{24,20},{28,24},{1,29},{... | collective-permute-start | bytes 3080 | tf_op jit(solution)/shard_map/ppermute | solution.py:26
  75.6 6.3 %collective-permute-start.4 = (bf16[2,256]{1,0:T(2,128)(2,1)S(1)}, bf16[2,256]{1,0:T(2,128)(2,1)S(1)}, u32[]{:S(2)}, u32[]{:S(2)}) collective-permute-start(bf16[2,256]{1,0:T(2,128)(2,1)S(1)} %collective-permute-done.2), channel_id=1, source_target_pairs={{0,4},{4,8},{8,12},{12,16},{16,20},{20,24},{24,28},{28,0},{1,5},{5... | collective-permute-start | bytes 3080 | tf_op jit(solution)/shard_map/ppermute | solution.py:23
  75.6 6.3 %collective-permute-start.5 = (bf16[2,256]{1,0:T(2,128)(2,1)S(1)}, bf16[2,256]{1,0:T(2,128)(2,1)S(1)}, u32[]{:S(2)}, u32[]{:S(2)}) collective-permute-start(bf16[2,256]{1,0:T(2,128)(2,1)S(1)} %collective-permute-done.3), channel_id=1, source_target_pairs={{0,28},{4,0},{8,4},{12,8},{16,12},{20,16},{24,20},{28,24},{1,29},{... | collective-permute-start | bytes 3080 | tf_op jit(solution)/shard_map/ppermute | solution.py:26
  81.8 6.3 %collective-permute-start.6 = (bf16[2,256]{1,0:T(2,128)(2,1)S(1)}, bf16[2,256]{1,0:T(2,128)(2,1)S(1)}, u32[]{:S(2)}, u32[]{:S(2)}) collective-permute-start(bf16[2,256]{1,0:T(2,128)(2,1)S(1)} %collective-permute-done.4), channel_id=1, source_target_pairs={{0,4},{4,8},{8,12},{12,16},{16,20},{20,24},{24,28},{28,0},{1,5},{5... | collective-permute-start | bytes 3080 | tf_op jit(solution)/shard_map/ppermute | solution.py:23
Sparse Core Ops, SparseCore 0:
  9.5 42.9 all-gather.2
